TPU v7x, 32 devices: a whole 2x2x4 slice. The times are simulated.
32 devices in a mesh: row: 2 (over y), col: 16 (over z, x, core).
Axes of the slice: x: 2, y: 2, z: 4, core: 2. Of those that a mesh axis runs over, the one named last changes fastest.
Arguments:
- queries: bfloat16 [8192, 1024], P(('row', 'col')), may hold values from -8 to 8
- key_rows: bfloat16 [8192, 1024], P(('row', 'col')), may hold values from -8 to 8
- value_rows: bfloat16 [8192, 1024], P(('row', 'col')), may hold values from -6 to 6
- out_grad: bfloat16 [8192, 1024], P(('row', 'col')), may hold values from -6 to 6
- dropout_bits: int32 [8192, 128], P(('row', 'col')), may hold values from 0 to 255, as said below
- partner: int32 [3, 2, 16], replicated, may hold values from 0 to 15, each once within a row
- block_pick: int32 [3, 2, 16], replicated, may hold values from 0 to 1
- global_blocks: int32 [2], replicated, may hold values from 0 to 63
Outputs:
- attended: bfloat16 [8192, 1024], P(('row', 'col'))
- query_grad: bfloat16 [8192, 1024], P(('row', 'col'))
- key_grad: bfloat16 [8192, 1024], P(('row', 'col'))
- value_grad: bfloat16 [8192, 1024], P(('row', 'col'))
Inputs may be any that keep to these rules, and one draw needn't show every extreme that they name: `dropout_bits`: each word packs 8 flags of 0 or 1 in its low bits. partner[r, a, :] is a permutation of the places 0 to 15.
All inputs are finite; a program needn't handle non-finite values.
Results may differ from a plain program's by a relative error of at most 0.0085.
Values may be sent and summed in bfloat16 or wider, within the bound.
A program may use at most 128 MiB of HBM per device.

v0:
```python
import jax
import jax.numpy as jnp
from jax import lax
from jax.sharding import PartitionSpec as P

HEADS = 16
HEAD_DIM = 64
BLOCK = 128
NGLOBAL = 2
NMATCH = 3
score_scale = 0.125
keep_scale = 1.0 / 0.9


def extended_2(value, sides, width):
    for axis, dim in sides:
        size, length = (lax.axis_size(axis), value.shape[dim])
        up = [(i, (i + 1) % size) for i in range(size)]
        down = [(j, i) for i, j in up]
        last = lax.slice_in_dim(value, length - width, length, axis=dim)
        leading = lax.slice_in_dim(value, 0, width, axis=dim)
        before = lax.ppermute(last, axis, up)
        after = lax.ppermute(leading, axis, down)
        value = jnp.concatenate([before, value, after], axis=dim)
    return value


def spread(value, axis, root):
    mine = lax.axis_index(axis) == root
    return lax.psum(jnp.where(mine, value, jnp.zeros_like(value)), axis)


def unpack_bits(packed):
    shifts = jnp.arange(8, dtype=jnp.int32)
    flags = jnp.right_shift(packed[..., None], shifts) & 1
    return flags.reshape(packed.shape[:-1] + (packed.shape[-1] * 8,))


def split_heads(array, lower, upper, group_heads):
    part_cols = array[..., lower:upper]
    return part_cols.reshape(
        part_cols.shape[:-1] + (group_heads, part_cols.shape[-1] // group_heads)
    )


def route_blocks(pieces_in, ordering):
    total_cols = lax.axis_size("col")
    matched, rows_in, channels = pieces_in.shape
    split_rows = pieces_in.reshape(matched, total_cols, rows_in // total_cols, channels)
    spread_out = lax.all_to_all(split_rows, "col", split_axis=1, concat_axis=1, tiled=True)
    arranged = jnp.stack([spread_out[matching][ordering[matching]] for matching in range(matched)])
    arrived = lax.all_to_all(arranged, "col", split_axis=1, concat_axis=1, tiled=True)
    return arrived.reshape(matched, rows_in, channels)


def route_all(pieces_in, ordering):
    return route_blocks(pieces_in, ordering)


def body(queries, key_rows, value_rows, out_grad, dropout_bits, partner, block_pick, global_blocks):
    tokens_here, model_width = queries.shape
    blocks_here = tokens_here // BLOCK
    group_heads = min(4, HEADS)
    group_width = group_heads * HEAD_DIM
    near_rows = 3 * BLOCK
    both_rows = jnp.concatenate([key_rows, value_rows], 1)
    band_index = lax.axis_index("row")
    place_index = lax.axis_index("col")
    total_cols = lax.axis_size("col")
    segment = band_index * total_cols + place_index
    extended = extended_2(both_rows, ((("row", "col"), 0),), BLOCK)
    shared_parts = []
    for global_slot in range(NGLOBAL):
        position = global_blocks[global_slot]
        source_piece = lax.dynamic_slice_in_dim(both_rows, position % blocks_here * BLOCK, BLOCK, 0)
        shared_parts.append(spread(source_piece, ("row", "col"), position // blocks_here))
    ordering = lax.dynamic_index_in_dim(partner, band_index, 1, keepdims=False)
    picks_row = lax.dynamic_index_in_dim(block_pick, band_index, 1, keepdims=False)
    col_ids = jnp.arange(total_cols, dtype=jnp.int32)
    inverse = jnp.sum(
        jnp.where(ordering[:, :, None] == col_ids[None, None, :], col_ids[None, :, None], 0), axis=1
    )
    askers = lax.dynamic_index_in_dim(inverse, place_index, 1, keepdims=False)
    wanted = jnp.take_along_axis(picks_row, askers[:, None], axis=1)[:, 0]
    outgoing = jnp.stack(
        [
            lax.dynamic_slice_in_dim(both_rows, wanted[matching] * BLOCK, BLOCK, 0)
            for matching in range(NMATCH)
        ]
    )
    fetched = route_all(outgoing, ordering)
    shared = jnp.concatenate(shared_parts + [fetched.reshape(NMATCH * BLOCK, 2 * model_width)], 0)
    windows = jnp.stack(
        [
            extended[start_block * BLOCK : start_block * BLOCK + near_rows]
            for start_block in range(blocks_here)
        ]
    )
    keep_mask = (unpack_bits(dropout_bits).astype(jnp.float32) * keep_scale).reshape(
        blocks_here, BLOCK, -1
    )
    keep_near = keep_mask[..., :near_rows][:, None]
    keep_far = keep_mask[..., near_rows:][:, None]
    query_blocks = queries.reshape(blocks_here, BLOCK, model_width)
    grad_blocks = out_grad.reshape(blocks_here, BLOCK, model_width)
    out_parts, query_parts = ([], [])
    key_near_parts, value_near_parts, key_far_parts, value_far_parts = ([], [], [], [])
    for group_index in range(HEADS // group_heads):
        lower = group_index * group_width
        upper = lower + group_width
        query_group = split_heads(query_blocks, lower, upper, group_heads)
        grad_group = split_heads(grad_blocks, lower, upper, group_heads)
        keys_near = split_heads(windows, lower, upper, group_heads)
        values_near = split_heads(windows, model_width + lower, model_width + upper, group_heads)
        keys_far = split_heads(shared, lower, upper, group_heads)
        values_far = split_heads(shared, model_width + lower, model_width + upper, group_heads)
        score_near = (
            jnp.einsum(
                "jqgd,jkgd->jgqk", query_group, keys_near, preferred_element_type=jnp.float32
            )
            * score_scale
        )
        score_far = (
            jnp.einsum("jqgd,kgd->jgqk", query_group, keys_far, preferred_element_type=jnp.float32)
            * score_scale
        )
        top = jnp.maximum(
            jnp.max(score_near, -1, keepdims=True), jnp.max(score_far, -1, keepdims=True)
        )
        total = jnp.sum(jnp.exp(score_near - top), -1, keepdims=True) + jnp.sum(
            jnp.exp(score_far - top), -1, keepdims=True
        )
        log_total = top + jnp.log(total)
        probs_near = jnp.exp(score_near - log_total)
        probs_far = jnp.exp(score_far - log_total)
        dropped_near = (probs_near * keep_near).astype(jnp.bfloat16)
        dropped_far = (probs_far * keep_far).astype(jnp.bfloat16)
        output_group = jnp.einsum(
            "jgqk,jkgd->jqgd", dropped_near, values_near, preferred_element_type=jnp.float32
        ) + jnp.einsum(
            "jgqk,kgd->jqgd", dropped_far, values_far, preferred_element_type=jnp.float32
        )
        out_parts.append(output_group.reshape(blocks_here, BLOCK, group_width))
        grad_near = (
            jnp.einsum(
                "jqgd,jkgd->jgqk", grad_group, values_near, preferred_element_type=jnp.float32
            )
            * keep_near
        )
        grad_far = (
            jnp.einsum("jqgd,kgd->jgqk", grad_group, values_far, preferred_element_type=jnp.float32)
            * keep_far
        )
        delta = jnp.sum(probs_near * grad_near, -1, keepdims=True) + jnp.sum(
            probs_far * grad_far, -1, keepdims=True
        )
        dscore_near = (probs_near * (grad_near - delta)).astype(jnp.bfloat16)
        dscore_far = (probs_far * (grad_far - delta)).astype(jnp.bfloat16)
        query_group_grad = score_scale * (
            jnp.einsum(
                "jgqk,jkgd->jqgd", dscore_near, keys_near, preferred_element_type=jnp.float32
            )
            + jnp.einsum("jgqk,kgd->jqgd", dscore_far, keys_far, preferred_element_type=jnp.float32)
        )
        query_parts.append(query_group_grad.reshape(blocks_here, BLOCK, group_width))
        key_near_parts.append(
            (
                score_scale
                * jnp.einsum(
                    "jgqk,jqgd->jkgd", dscore_near, query_group, preferred_element_type=jnp.float32
                )
            ).reshape(blocks_here, near_rows, group_width)
        )
        value_near_parts.append(
            jnp.einsum(
                "jgqk,jqgd->jkgd", dropped_near, grad_group, preferred_element_type=jnp.float32
            ).reshape(blocks_here, near_rows, group_width)
        )
        key_far_parts.append(
            (
                score_scale
                * jnp.einsum(
                    "jgqk,jqgd->kgd", dscore_far, query_group, preferred_element_type=jnp.float32
                )
            ).reshape(-1, group_width)
        )
        value_far_parts.append(
            jnp.einsum(
                "jgqk,jqgd->kgd", dropped_far, grad_group, preferred_element_type=jnp.float32
            ).reshape(-1, group_width)
        )
    attended = jnp.concatenate(out_parts, -1).astype(jnp.bfloat16).reshape(tokens_here, model_width)
    query_grad = (
        jnp.concatenate(query_parts, -1).astype(jnp.bfloat16).reshape(tokens_here, model_width)
    )
    near_grads = jnp.concatenate(key_near_parts + value_near_parts, -1)
    far_grads = jnp.concatenate(key_far_parts + value_far_parts, -1)
    window_total = jnp.zeros((tokens_here + 2 * BLOCK, 2 * model_width), jnp.float32)
    for start_block in range(blocks_here):
        window_total = window_total.at[start_block * BLOCK : start_block * BLOCK + near_rows].add(
            near_grads[start_block]
        )
    rims = jnp.concatenate([window_total[:BLOCK], window_total[-BLOCK:]], 0).astype(jnp.bfloat16)
    returned = extended_2(rims, ((("row", "col"), 0),), BLOCK)
    gradients = window_total[BLOCK : BLOCK + tokens_here]
    gradients = gradients.at[:BLOCK].add(returned[:BLOCK].astype(jnp.float32))
    gradients = gradients.at[tokens_here - BLOCK :].add(returned[3 * BLOCK :].astype(jnp.float32))
    global_sum = lax.psum(far_grads[: NGLOBAL * BLOCK], ("row", "col"))
    for global_slot in range(NGLOBAL):
        position = global_blocks[global_slot]
        owner_here = position // blocks_here == segment
        row_offset = position % blocks_here * BLOCK
        current = lax.dynamic_slice_in_dim(gradients, row_offset, BLOCK, 0)
        addition = jnp.where(
            owner_here, global_sum[global_slot * BLOCK : (global_slot + 1) * BLOCK], 0.0
        )
        gradients = lax.dynamic_update_slice_in_dim(gradients, current + addition, row_offset, 0)
    random_grads = (
        far_grads[NGLOBAL * BLOCK :].reshape(NMATCH, BLOCK, 2 * model_width).astype(jnp.bfloat16)
    )
    came_back = route_all(random_grads, inverse)
    for matching in range(NMATCH):
        row_offset = wanted[matching] * BLOCK
        current = lax.dynamic_slice_in_dim(gradients, row_offset, BLOCK, 0)
        gradients = lax.dynamic_update_slice_in_dim(
            gradients, current + came_back[matching].astype(jnp.float32), row_offset, 0
        )
    return (
        attended,
        query_grad,
        gradients[:, :model_width].astype(jnp.bfloat16),
        gradients[:, model_width:].astype(jnp.bfloat16),
    )


def solution(mesh):
    in_specs = (
        P(("row", "col"), None),
        P(("row", "col"), None),
        P(("row", "col"), None),
        P(("row", "col"), None),
        P(("row", "col"), None),
        P(),
        P(),
        P(),
    )
    out_specs = (
        P(("row", "col"), None),
        P(("row", "col"), None),
        P(("row", "col"), None),
        P(("row", "col"), None),
    )
    return jax.shard_map(body, mesh=mesh, in_specs=in_specs, out_specs=out_specs, check_vma=False)
```

profile of v0, /device:TPU:0, one launch (start us, length us, event | category | flops | bytes accessed | tf_op | source)
XLA Modules:
  0.0 565.9 jit_solution(7647314221902579277)
XLA Ops:
  22.5 7.5 %all-to-all-start = ((bf16[3,16,8,2048]{3,2,0,1:T(8,128)(2,1)}), bf16[3,16,8,2048]{3,2,0,1:T(8,128)(2,1)S(1)}, u32[]{:S(2)}, u32[]{:S(2)}) async-start(bf16[3,16,8,2048]{3,2,0,1:T(8,128)(2,1)} %pad_maximum_fusion.1), calls=%async_computation | async-start | bytes 3145728 | tf_op jit(solution)/shard_map/all_to_all | solution.py:50
  30.1 31.8 %all-to-all-done = bf16[3,16,8,2048]{3,2,0,1:T(8,128)(2,1)S(1)} async-done(((bf16[3,16,8,2048]{3,2,0,1:T(8,128)(2,1)}), bf16[3,16,8,2048]{3,2,0,1:T(8,128)(2,1)S(1)}, u32[]{:S(2)}, u32[]{:S(2)}) %all-to-all-start) | async-done | bytes 1572896 | tf_op jit(solution)/shard_map/all_to_all | solution.py:50
  63.1 1.6 gather_fusion
  64.7 1.6 gather_fusion.1
  68.3 9.3 %all-to-all-start.1 = ((bf16[3,16,8,2048]{3,2,0,1:T(8,128)(2,1)}), bf16[3,16,8,2048]{3,2,0,1:T(8,128)(2,1)}, u32[]{:S(2)}, u32[]{:S(2)}) async-start(bf16[3,16,8,2048]{3,2,0,1:T(8,128)(2,1)} %copy.750), calls=%async_computation.1 | async-start | bytes 3145728 | tf_op jit(solution)/shard_map/all_to_all | solution.py:52
  78.1 5.0 collective-permute-start.1
  83.9 3.5 convert_multiply_fusion
  95.9 23.3 %collective-permute-done = bf16[128,2048]{1,0:T(8,128)(2,1)} collective-permute-done((bf16[128,2048]{1,0:T(8,128)(2,1)}, bf16[128,2048]{1,0:T(8,128)(2,1)}, u32[]{:S(2)}, u32[]{:S(2)}) %collective-permute-start) | collective-permute-done | bytes 524320 | tf_op jit(solution)/shard_map/ppermute | solution.py:22
  121.9 1.9 copy.741
  129.2 1.6 bitcast_reduce_fusion.5
  132.9 2.7 copy.751
  135.7 93.7 %all-reduce.7.cloned.1.call-done = (bf16[128,2048]{1,0:T(8,128)(2,1)}, bf16[128,2048]{1,0:T(8,128)(2,1)}) async-done(((bf16[128,2048]{1,0:T(8,128)(2,1)}, bf16[128,2048]{1,0:T(8,128)(2,1)}), (bf16[128,2048]{1,0:T(8,128)(2,1)}, bf16[128,2048]{1,0:T(8,128)(2,1)})) %all-reduce.7.cloned.1.call-update) | async-done | bytes 1048592 | tf_op jit(solution)/shard_map/psum | solution.py:30
  229.4 2.0 pad_maximum_fusion
  233.0 1.9 copy.752
  234.8 1.9 copy.800
  236.7 1.9 copy.794
  238.6 1.9 copy.787
  240.5 1.9 copy.781
  242.3 1.9 copy.774
  244.2 1.9 copy.768
  246.1 1.9 copy.760
  247.9 1.7 bitcast_reduce_fusion.2
  262.1 1.8 multiply_reduce_fusion.6
  263.9 1.7 multiply_reduce_fusion.5
  265.7 1.7 multiply_reduce_fusion.4
  270.5 1.7 multiply_reduce_fusion.7
  272.3 3.9 multiply_reduce_fusion.3
  278.0 7.7 %multiply_convert_fusion.3 = (bf16[2,4,128,640]{2,3,0,1:T(8,128)(2,1)}, bf16[2,4,128,640]{2,3,0,1:T(8,128)(2,1)}, bf16[2,4,128,640]{2,3,0,1:T(8,128)(2,1)}, bf16...) fusion(f32[4,640,2,128]{3,1,2,0:T(8,128)} %get-tuple-element.16, ...), kind=kLoop, calls=%fused_computation.61 | loop fusion | flops 20971520 | bytes 32145408 | tf_op jit(solution)/shard_map/convert_element_type | solution.py:158
  285.8 2.7 fusion.41
  288.5 2.2 copy.864
  290.7 2.7 fusion.42
  293.3 2.2 copy.865
  295.5 2.7 fusion.43
  298.2 2.2 copy.866
  300.4 2.7 fusion.44
  303.0 2.2 copy.867
  305.2 2.7 fusion.118
  307.9 2.2 copy.868
  310.0 2.6 fusion.114
  312.7 2.2 copy.869
  314.8 2.7 fusion.110
  317.5 2.1 copy.870
  319.6 2.7 fusion.106
  322.3 2.2 copy.871
  332.2 2.3 copy.845
  334.4 2.3 copy.846
  336.7 2.3 copy.847
  339.0 2.3 copy.844
  341.3 2.3 multiply_convert_fusion.9
  373.0 2.3 copy.842
  378.4 4.7 all-to-all-start.2
  395.1 2.6 copy-done.15
  397.9 21.7 %all-to-all-done.2 = bf16[3,16,8,2048]{3,2,0,1:T(8,128)(2,1)} async-done(((bf16[3,16,8,2048]{3,2,0,1:T(8,128)(2,1)}), bf16[3,16,8,2048]{3,2,0,1:T(8,128)(2,1)}, u32[]{:S(2)}, u32[]{:S(2)}) %all-to-all-start.2) | async-done | bytes 1572896 | tf_op jit(solution)/shard_map/all_to_all | solution.py:50
  419.6 2.5 slice_bitcast_fusion.7
  422.1 2.5 gather_fusion.3
  424.7 2.5 gather_fusion.5
  427.2 2.5 gather_fusion.4
  432.5 13.6 %all-to-all-start.3 = ((bf16[3,16,8,2048]{3,2,0,1:T(8,128)(2,1)}), bf16[3,16,8,2048]{3,2,0,1:T(8,128)(2,1)}, u32[]{:S(2)}, u32[]{:S(2)}) async-start(bf16[3,16,8,2048]{3,2,0,1:T(8,128)(2,1)} %copy.873), calls=%async_computation.3 | async-start | bytes 3145728 | tf_op jit(solution)/shard_map/all_to_all | solution.py:52
  446.1 2.5 fusion
  449.9 2.5 fusion.98
  452.5 4.6 collective-permute-start.3
  459.5 24.8 %collective-permute-done.2 = bf16[128,2048]{1,0:T(8,128)(2,1)} collective-permute-done((bf16[128,2048]{1,0:T(8,128)(2,1)}, bf16[128,2048]{1,0:T(8,128)(2,1)}, u32[]{:S(2)}, u32[]{:S(2)}) %collective-permute-start.2) | collective-permute-done | bytes 524320 | tf_op jit(solution)/shard_map/ppermute | solution.py:22
  487.1 64.7 %all-reduce.5.cloned.1.call-done = f32[256,2048]{1,0:T(8,128)} async-done(((f32[256,2048]{1,0:T(8,128)}), f32[256,2048]{1,0:T(8,128)}) %all-reduce.5.cloned.1.call-update) | async-done | bytes 2097168 | tf_op jit(solution)/shard_map/psum | solution.py:208
  551.8 1.6 fusion.92
  (405 shorter events, 115.8 us)
Async XLA Ops:
  7.2 6.6 %copy-start = (s32[3,2,16]{2,1,0:T(2,128)S(1)}, s32[3,2,16]{2,1,0:T(2,128)}, u32[]{:S(2)}) copy-start(s32[3,2,16]{2,1,0:T(2,128)} %param.22) | copy-start | bytes 1156
  7.2 12.4 %copy-start.84 = (bf16[256,1024]{1,0:T(8,128)(2,1)S(1)}, bf16[256,1024]{1,0:T(8,128)(2,1)}, u32[]{:S(2)}) copy-start(bf16[256,1024]{1,0:T(8,128)(2,1)} %param.18) | copy-start | bytes 1572868
  22.5 7.5 %copy-start.104 = (s32[3,2,16]{2,1,0:T(2,128)S(1)}, s32[3,2,16]{2,1,0:T(2,128)}, u32[]{:S(2)}) copy-start(s32[3,2,16]{2,1,0:T(2,128)} %param.21) | copy-start | bytes 1156
  22.5 39.4 %all-to-all-start = ((bf16[3,16,8,2048]{3,2,0,1:T(8,128)(2,1)}), bf16[3,16,8,2048]{3,2,0,1:T(8,128)(2,1)S(1)}, u32[]{:S(2)}, u32[]{:S(2)}) async-start(bf16[3,16,8,2048]{3,2,0,1:T(8,128)(2,1)} %pad_maximum_fusion.1), calls=%async_computation | async-start | bytes 3145728 | tf_op jit(solution)/shard_map/all_to_all | solution.py:50
  68.3 14.9 %copy-start.95 = (s32[256,128]{1,0:T(8,128)S(1)}, s32[256,128]{1,0:T(8,128)}, u32[]{:S(2)}) copy-start(s32[256,128]{1,0:T(8,128)} %param.20) | copy-start | bytes 393220
  68.3 64.6 %all-to-all-start.1 = ((bf16[3,16,8,2048]{3,2,0,1:T(8,128)(2,1)}), bf16[3,16,8,2048]{3,2,0,1:T(8,128)(2,1)}, u32[]{:S(2)}, u32[]{:S(2)}) async-start(bf16[3,16,8,2048]{3,2,0,1:T(8,128)(2,1)} %copy.750), calls=%async_computation.1 | async-start | bytes 3145728 | tf_op jit(solution)/shard_map/all_to_all | solution.py:52
  77.6 151.8 %all-reduce.7.cloned.1.call-start = ((), (), s32[]{:S(2)}) async-start(), calls=%async_computation.5 | async-start | bytes 2097152 | tf_op jit(solution)/shard_map/psum | solution.py:30
  77.7 41.5 %collective-permute-start = (bf16[128,2048]{1,0:T(8,128)(2,1)}, bf16[128,2048]{1,0:T(8,128)(2,1)}, u32[]{:S(2)}, u32[]{:S(2)}) collective-permute-start(bf16[128,2048]{1,0:T(8,128)(2,1)} %get-tuple-element.116), channel_id=1, source_target_pairs={{0,1},{1,2},{2,3},{3,4},{4,5},{5,6},{6,7},{7,8},{8,9},{9,10},{10,1... | collective-permute-start | bytes 1572872 | tf_op jit(solution)/shard_map/ppermute | solution.py:22
  78.1 41.1 %collective-permute-start.1 = (bf16[128,2048]{1,0:T(8,128)(2,1)}, bf16[128,2048]{1,0:T(8,128)(2,1)}, u32[]{:S(2)}, u32[]{:S(2)}) collective-permute-start(bf16[128,2048]{1,0:T(8,128)(2,1)} %get-tuple-element.122), channel_id=1, source_target_pairs={{1,0},{2,1},{3,2},{4,3},{5,4},{6,5},{7,6},{8,7},{9,8},{10,9},{11,1... | collective-permute-start | bytes 1572872 | tf_op jit(solution)/shard_map/ppermute | solution.py:23
  87.5 2.7 copy-start.86
  89.0 4.3 slice-start
  89.9 39.3 %copy-start.50 = (bf16[2,128,256]{1,2,0:T(8,128)(2,1)}, bf16[2,128,256]{1,2,0:T(8,128)(2,1)S(1)}, u32[]{:S(2)}) copy-start(bf16[2,128,256]{1,2,0:T(8,128)(2,1)S(1)} %copy.941) | copy-start | bytes 393220
  90.0 40.9 %copy-start.48 = (bf16[2,128,256]{1,2,0:T(8,128)(2,1)}, bf16[2,128,256]{1,2,0:T(8,128)(2,1)S(1)}, u32[]{:S(2)}) copy-start(bf16[2,128,256]{1,2,0:T(8,128)(2,1)S(1)} %copy.940) | copy-start | bytes 393220
  90.0 3.2 slice-start.1
  90.2 38.0 %copy-start.42 = (bf16[2,128,256]{1,2,0:T(8,128)(2,1)}, bf16[2,128,256]{1,2,0:T(8,128)(2,1)S(1)}, u32[]{:S(2)}) copy-start(bf16[2,128,256]{1,2,0:T(8,128)(2,1)S(1)} %copy.942) | copy-start | bytes 393220
  125.9 5.0 copy-start.26
  127.0 2.2 copy-start.28
  127.3 3.6 copy-start.22
  255.0 1.9 copy-start.67
  259.2 1.8 copy-start.69
  262.1 1.8 copy-start.36
  263.9 1.7 copy-start.30
  265.7 1.7 copy-start.46
  265.7 1.7 copy-start.62
  268.7 1.9 copy-start.32
  270.5 1.7 copy-start.20
  270.5 1.7 copy-start.73
  276.2 9.6 %copy-start.96 = (f32[2,4,128]{2,1,0:T(4,128)}, f32[2,4,128]{2,1,0:T(4,128)S(1)}, u32[]{:S(2)}) copy-start(f32[2,4,128]{2,1,0:T(4,128)S(1)} %copy_add_fusion) | copy-start | bytes 12292
  276.8 8.9 %copy-start.98 = (f32[2,4,128]{2,1,0:T(4,128)}, f32[2,4,128]{2,1,0:T(4,128)S(1)}, u32[]{:S(2)}) copy-start(f32[2,4,128]{2,1,0:T(4,128)S(1)} %copy_add_fusion.2) | copy-start | bytes 12292
  277.4 8.3 %copy-start.101 = (f32[2,4,128]{2,1,0:T(4,128)}, f32[2,4,128]{2,1,0:T(4,128)S(1)}, u32[]{:S(2)}) copy-start(f32[2,4,128]{2,1,0:T(4,128)S(1)} %copy_add_fusion.3) | copy-start | bytes 12292
  341.3 2.4 copy-start.19
  341.3 2.4 copy-start.102
  343.7 1.9 copy-start.18
  343.7 1.9 copy-start.99
  345.9 2.1 copy-start.13
  345.9 2.1 copy-start.72
  348.0 1.8 copy-start.29
  348.4 2.3 copy-start.12
  348.4 2.3 copy-start.68
  352.7 2.1 copy-start.27
  353.3 2.4 copy-start.10
  353.3 2.4 copy-start.65
  361.8 6.3 %copy-start.60 = (f32[2,4,384,64]{2,3,1,0:T(8,128)S(1)}, f32[2,4,384,64]{2,3,1,0:T(8,128)}, u32[]{:S(2)}) copy-start(f32[2,4,384,64]{2,3,1,0:T(8,128)} %convolution_multiply_fusion.6) | copy-start | bytes 2359300
  369.3 7.8 %copy-start.16 = (bf16[384,2048]{1,0:T(8,128)(2,1)S(1)}, bf16[384,2048]{1,0:T(8,128)(2,1)}, u32[]{:S(2)}) copy-start(bf16[384,2048]{1,0:T(8,128)(2,1)} %slice.504) | copy-start | bytes 4718596
  378.4 4.8 copy-start.31
  378.4 4.8 copy-start.83
  378.4 41.2 %all-to-all-start.2 = ((bf16[3,16,8,2048]{3,2,0,1:T(8,128)(2,1)}), bf16[3,16,8,2048]{3,2,0,1:T(8,128)(2,1)}, u32[]{:S(2)}, u32[]{:S(2)}) async-start(bf16[3,16,8,2048]{3,2,0,1:T(8,128)(2,1)} %copy.872), calls=%async_computation.2 | async-start | bytes 3145728 | tf_op jit(solution)/shard_map/all_to_all | solution.py:50
  383.1 168.6 %all-reduce.5.cloned.1.call-start = ((), (), s32[]{:S(2)}) async-start(), calls=%async_computation.4 | async-start | bytes 4194304 | tf_op jit(solution)/shard_map/psum | solution.py:208
  385.5 2.8 copy-start.7
  386.9 2.8 copy-start.23
  395.0 2.6 copy-start.15
  432.5 121.4 %all-to-all-start.3 = ((bf16[3,16,8,2048]{3,2,0,1:T(8,128)(2,1)}), bf16[3,16,8,2048]{3,2,0,1:T(8,128)(2,1)}, u32[]{:S(2)}, u32[]{:S(2)}) async-start(bf16[3,16,8,2048]{3,2,0,1:T(8,128)(2,1)} %copy.873), calls=%async_computation.3 | async-start | bytes 3145728 | tf_op jit(solution)/shard_map/all_to_all | solution.py:52
  448.6 8.6 %copy-start.6 = (f32[384,2048]{1,0:T(8,128)}, f32[384,2048]{1,0:T(8,128)S(1)}, u32[]{:S(2)}) copy-start(f32[384,2048]{1,0:T(8,128)S(1)} %fusion) | copy-start | bytes 9437188
  448.6 8.4 %copy-start.88 = (bf16[32,8,2,128]{3,1,2,0:T(8,128)(2,1)S(1)}, bf16[32,8,2,128]{3,1,2,0:T(8,128)(2,1)}, u32[]{:S(2)}) copy-start(bf16[32,8,2,128]{3,1,2,0:T(8,128)(2,1)} %copy.1074) | copy-start | bytes 393220
  448.7 8.4 %copy-start.89 = (bf16[32,8,2,128]{3,1,2,0:T(8,128)(2,1)S(1)}, bf16[32,8,2,128]{3,1,2,0:T(8,128)(2,1)}, u32[]{:S(2)}) copy-start(bf16[32,8,2,128]{3,1,2,0:T(8,128)(2,1)} %copy.1073) | copy-start | bytes 393220
  448.7 8.4 %copy-start.91 = (bf16[32,8,2,128]{3,1,2,0:T(8,128)(2,1)S(1)}, bf16[32,8,2,128]{3,1,2,0:T(8,128)(2,1)}, u32[]{:S(2)}) copy-start(bf16[32,8,2,128]{3,1,2,0:T(8,128)(2,1)} %copy.1072) | copy-start | bytes 393220
  448.7 8.4 %copy-start.93 = (bf16[32,8,2,128]{3,1,2,0:T(8,128)(2,1)S(1)}, bf16[32,8,2,128]{3,1,2,0:T(8,128)(2,1)}, u32[]{:S(2)}) copy-start(bf16[32,8,2,128]{3,1,2,0:T(8,128)(2,1)} %copy.1071) | copy-start | bytes 393220
  448.7 8.5 %copy-start.87 = (bf16[32,8,2,128]{3,1,2,0:T(8,128)(2,1)S(1)}, bf16[32,8,2,128]{3,1,2,0:T(8,128)(2,1)}, u32[]{:S(2)}) copy-start(bf16[32,8,2,128]{3,1,2,0:T(8,128)(2,1)} %copy.1070) | copy-start | bytes 393220
  448.7 8.5 %copy-start.90 = (bf16[32,8,2,128]{3,1,2,0:T(8,128)(2,1)S(1)}, bf16[32,8,2,128]{3,1,2,0:T(8,128)(2,1)}, u32[]{:S(2)}) copy-start(bf16[32,8,2,128]{3,1,2,0:T(8,128)(2,1)} %copy.1069) | copy-start | bytes 393220
  448.7 8.5 %copy-start.92 = (bf16[32,8,2,128]{3,1,2,0:T(8,128)(2,1)S(1)}, bf16[32,8,2,128]{3,1,2,0:T(8,128)(2,1)}, u32[]{:S(2)}) copy-start(bf16[32,8,2,128]{3,1,2,0:T(8,128)(2,1)} %copy.1068) | copy-start | bytes 393220
  448.7 8.5 %copy-start.94 = (bf16[32,8,2,128]{3,1,2,0:T(8,128)(2,1)S(1)}, bf16[32,8,2,128]{3,1,2,0:T(8,128)(2,1)}, u32[]{:S(2)}) copy-start(bf16[32,8,2,128]{3,1,2,0:T(8,128)(2,1)} %copy.1067) | copy-start | bytes 393220
  449.6 34.7 %collective-permute-start.2 = (bf16[128,2048]{1,0:T(8,128)(2,1)}, bf16[128,2048]{1,0:T(8,128)(2,1)}, u32[]{:S(2)}, u32[]{:S(2)}) collective-permute-start(bf16[128,2048]{1,0:T(8,128)(2,1)} %slice.505), channel_id=1, source_target_pairs={{0,1},{1,2},{2,3},{3,4},{4,5},{5,6},{6,7},{7,8},{8,9},{9,10},{10,1... | collective-permute-start | bytes 1572872 | tf_op jit(solution)/shard_map/ppermute | solution.py:22
  452.5 33.3 %collective-permute-start.3 = (bf16[128,2048]{1,0:T(8,128)(2,1)}, bf16[128,2048]{1,0:T(8,128)(2,1)}, u32[]{:S(2)}, u32[]{:S(2)}) collective-permute-start(bf16[128,2048]{1,0:T(8,128)(2,1)} %fusion.98), channel_id=1, source_target_pairs={{1,0},{2,1},{3,2},{4,3},{5,4},{6,5},{7,6},{8,7},{9,8},{10,9},{11,1... | collective-permute-start | bytes 1572872 | tf_op jit(solution)/shard_map/ppermute | solution.py:23
  551.8 1.9 copy-start.82
  (53 other events, 65.3 us)
Sparse Core Ops, SparseCore 0:
  84.4 144.9 all-reduce.6
  391.0 160.7 all-reduce.4
where the time goes:
time: 572 us; the launch traced here: 566 us
  waiting for transfers between devices  260 us (45%)
  local copies, waits for them, and re-layouts  133 us (23%)
  matrix products  64.1 us (11%)
  starting transfers between devices  45.6 us (8%)
  other arithmetic  39.9 us (7%)
  between operations  23.1 us (4%)
    psum x1, waiting for transfers between devices, spread(): return lax.psum(jnp.where(mine, value, jnp.zeros_like(value)), axis)  93.7 us
    psum x1, waiting for transfers between devices, body(): global_sum = lax.psum(far_grads[:NGLOBAL * BLOCK], ('row', 'col'))  64.7 us
    all_to_all x2, waiting for transfers between devices, route_blocks(): lax.all_to_all(split_rows, 'col', split_axis=1, concat_axis=1, tiled=True)  53.5 us
    ppermute x2, waiting for transfers between devices, extended_2(): before = lax.ppermute(last, axis, up)  48.1 us
    unnamed x249, local copies, waits for them, and re-layouts  35.2 us
    all_to_all x2, starting transfers between devices, route_blocks(): lax.all_to_all(arranged, 'col', split_axis=1, concat_axis=1, tiled=True)  22.9 us
    slice x19, local copies, waits for them, and re-layouts, split_heads(): part_cols = array[..., lower:upper]  22.8 us
    all_to_all x2, starting transfers between devices, route_blocks(): lax.all_to_all(split_rows, 'col', split_axis=1, concat_axis=1, tiled=True)  12.3 us
  transfers between devices with their start and end apart: 10, of which 6 were waited for; matrix products, arithmetic and copies ran while one was open for 11% of the time, Pallas kernels for 0%

commit v1 on v0

--- a/solution.py
+++ b/solution.py
@@ -205,7 +205,9 @@
     gradients = window_total[BLOCK : BLOCK + tokens_here]
     gradients = gradients.at[:BLOCK].add(returned[:BLOCK].astype(jnp.float32))
     gradients = gradients.at[tokens_here - BLOCK :].add(returned[3 * BLOCK :].astype(jnp.float32))
-    global_sum = lax.psum(far_grads[: NGLOBAL * BLOCK], ("row", "col"))
+    part = far_grads[: NGLOBAL * BLOCK]
+    shards = lax.all_gather(part, ("row", "col"))
+    global_sum = jnp.sum(shards, axis=0)
     for global_slot in range(NGLOBAL):
         position = global_blocks[global_slot]
         owner_here = position // blocks_here == segment

time: 572 us -> 809 us (1.41)
  waiting for transfers between devices: 260 us -> 455 us
  other arithmetic: 39.9 us -> 61 us
  starting transfers between devices: 45.6 us -> 55 us
    all_gather x0 -> x1, waiting for transfers between devices: none -> 244 us  [body(): shards = lax.all_gather(part, ('row', 'col'))]
    psum x1 -> x0, waiting for transfers between devices: 64.7 us -> none  [body(): global_sum = lax.psum(far_grads[:NGLOBAL * BLOCK], ('row', 'col'))]
    ppermute x2, waiting for transfers between devices: 48.1 us -> 84.5 us  [extended_2(): before = lax.ppermute(last, axis, up)]
    reduce_sum x0 -> x1, other arithmetic: none -> 22.3 us  [body(): global_sum = jnp.sum(shards, axis=0)]
    all_to_all x2, waiting for transfers between devices: 53.5 us -> 35.6 us  [route_blocks(): lax.all_to_all(split_rows, 'col', split_axis=1, concat_axis=1, tiled=True)]
    all_to_all x2, starting transfers between devices: 22.9 us -> 31.9 us  [route_blocks(): lax.all_to_all(arranged, 'col', split_axis=1, concat_axis=1, tiled=True)]
    unnamed x249 -> x269, local copies, waits for them, and re-layouts: 35.2 us -> 42.5 us
  transfers between devices with their start and end apart: 10 -> 10, of which waited for: 6 -> 6; matrix products, arithmetic and copies ran while one was open for 11% -> 15% of each run, Pallas kernels for 0% -> 0%
where the time goes in v1:
time: 809 us; the launch traced here: 803 us
  waiting for transfers between devices  455 us (56%)
  local copies, waits for them, and re-layouts  139 us (17%)
  matrix products  69.7 us (9%)
  other arithmetic  61 us (8%)
  starting transfers between devices  55 us (7%)
  between operations  22.8 us (3%)
    all_gather x1, waiting for transfers between devices, body(): shards = lax.all_gather(part, ('row', 'col'))  244 us
    psum x1, waiting for transfers between devices, spread(): return lax.psum(jnp.where(mine, value, jnp.zeros_like(value)), axis)  90.8 us
    ppermute x2, waiting for transfers between devices, extended_2(): before = lax.ppermute(last, axis, up)  84.5 us
    unnamed x269, local copies, waits for them, and re-layouts  42.5 us
    all_to_all x2, waiting for transfers between devices, route_blocks(): lax.all_to_all(split_rows, 'col', split_axis=1, concat_axis=1, tiled=True)  35.6 us
    all_to_all x2, starting transfers between devices, route_blocks(): lax.all_to_all(arranged, 'col', split_axis=1, concat_axis=1, tiled=True)  31.9 us
    slice x19, local copies, waits for them, and re-layouts, split_heads(): part_cols = array[..., lower:upper]  26.4 us
    reduce_sum x1, other arithmetic, body(): global_sum = jnp.sum(shards, axis=0)  22.3 us
  transfers between devices with their start and end apart: 10, of which 6 were waited for; matrix products, arithmetic and copies ran while one was open for 15% of the time, Pallas kernels for 0%

profile of v1, /device:TPU:0, one launch (start us, length us, event | category | flops | bytes accessed | tf_op | source)
XLA Modules:
  0.0 802.5 jit_solution(8017639387991613444)
XLA Ops:
  22.8 7.5 all-to-all-start
  31.0 31.2 %all-to-all-done = bf16[3,16,8,2048]{3,2,0,1:T(8,128)(2,1)S(1)} async-done(((bf16[3,16,8,2048]{3,2,0,1:T(8,128)(2,1)}), bf16[3,16,8,2048]{3,2,0,1:T(8,128)(2,1)S(1)}, u32[]{:S(2)}, u32[]{:S(2)}) %all-to-all-start) | async-done | bytes 1572896 | tf_op jit(solution)/shard_map/all_to_all | solution.py:50
  68.6 9.3 %all-to-all-start.1 = ((bf16[3,16,8,2048]{3,2,0,1:T(8,128)(2,1)}), bf16[3,16,8,2048]{3,2,0,1:T(8,128)(2,1)}, u32[]{:S(2)}, u32[]{:S(2)}) async-start(bf16[3,16,8,2048]{3,2,0,1:T(8,128)(2,1)} %copy.632), calls=%async_computation.1 | async-start | bytes 3145728 | tf_op jit(solution)/shard_map/all_to_all | solution.py:52
  78.4 5.0 collective-permute-start.1
  84.3 3.8 convert_multiply_fusion
  96.6 22.9 %collective-permute-done = bf16[128,2048]{1,0:T(8,128)(2,1)} collective-permute-done((bf16[128,2048]{1,0:T(8,128)(2,1)}, bf16[128,2048]{1,0:T(8,128)(2,1)}, u32[]{:S(2)}, u32[]{:S(2)}) %collective-permute-start) | collective-permute-done | bytes 524320 | tf_op jit(solution)/shard_map/ppermute | solution.py:22
  124.1 2.1 copy.674
  126.2 1.9 copy.623
  136.1 2.7 copy.633
  138.9 90.8 %all-reduce.4.cloned.1.call-done = (bf16[128,2048]{1,0:T(8,128)(2,1)}, bf16[128,2048]{1,0:T(8,128)(2,1)}) async-done(((bf16[128,2048]{1,0:T(8,128)(2,1)}, bf16[128,2048]{1,0:T(8,128)(2,1)}), (bf16[128,2048]{1,0:T(8,128)(2,1)}, bf16[128,2048]{1,0:T(8,128)(2,1)})) %all-reduce.4.cloned.1.call-update) | async-done | bytes 1048592 | tf_op jit(solution)/shard_map/psum | solution.py:30
  229.7 2.0 pad_maximum_fusion
  233.3 1.9 copy.682
  235.1 1.9 copy.634
  237.0 1.7 bitcast_reduce_fusion.3
  240.8 1.9 copy.656
  242.6 1.9 copy.650
  244.5 1.7 bitcast_reduce_fusion.2
  248.4 1.9 copy.669
  250.3 1.9 copy.663
  255.8 1.9 copy.676
  261.4 1.9 copy.642
  263.2 1.7 fusion.116
  265.0 1.9 fusion.112
  266.9 1.7 fusion.108
  268.6 1.7 multiply_reduce_fusion.7
  271.0 5.1 multiply_reduce_fusion.3
  276.2 1.7 multiply_reduce_fusion.6
  278.0 1.7 multiply_reduce_fusion.5
  279.7 1.7 multiply_reduce_fusion.4
  281.4 7.5 multiply_convert_fusion.3
  288.9 2.7 fusion.41
  291.6 2.1 copy.746
  293.8 2.2 constant_dynamic-update-slice_fusion.17
  295.9 2.3 fusion.42
  298.2 2.1 copy.747
  300.3 2.7 fusion.43
  303.0 2.2 copy.748
  305.2 2.7 fusion.44
  307.9 2.2 copy.749
  310.1 2.7 fusion.118
  312.7 2.2 copy.750
  315.0 2.7 fusion.114
  317.6 2.2 copy.751
  319.8 2.7 fusion.110
  322.5 2.2 copy.752
  324.6 2.7 fusion.106
  327.3 2.2 copy.753
  329.5 2.1 constant_dynamic-update-slice_fusion.16
  337.3 3.1 slice.404
  344.3 2.1 slice.504
  347.7 4.8 all-to-all-start.2
  352.5 1.9 fusion.78
  385.7 2.4 copy.723
  404.8 4.3 all-to-all-done.2
  409.1 2.6 slice_bitcast_fusion.7
  411.7 2.5 gather_fusion.5
  414.3 2.5 gather_fusion.4
  416.8 2.5 gather_fusion.3
  422.1 22.6 %all-to-all-start.3 = ((bf16[3,16,8,2048]{3,2,0,1:T(8,128)(2,1)}), bf16[3,16,8,2048]{3,2,0,1:T(8,128)(2,1)}, u32[]{:S(2)}, u32[]{:S(2)}) async-start(bf16[3,16,8,2048]{3,2,0,1:T(8,128)(2,1)} %copy.758), calls=%async_computation.3 | async-start | bytes 3145728 | tf_op jit(solution)/shard_map/all_to_all | solution.py:52
  447.7 2.3 fusion.98
  450.0 5.0 collective-permute-start.3
  457.3 61.6 %collective-permute-done.2 = bf16[128,2048]{1,0:T(8,128)(2,1)} collective-permute-done((bf16[128,2048]{1,0:T(8,128)(2,1)}, bf16[128,2048]{1,0:T(8,128)(2,1)}, u32[]{:S(2)}, u32[]{:S(2)}) %collective-permute-start.2) | collective-permute-done | bytes 524320 | tf_op jit(solution)/shard_map/ppermute | solution.py:22
  521.7 244.4 %all-gather.3.cloned.1.call-done = f32[8192,2048]{1,0:T(8,128)} async-done(((f32[256,2048]{1,0:T(8,128)}), f32[8192,2048]{1,0:T(8,128)}) %all-gather.3.cloned.1.call-update) | async-done | bytes 67108880 | tf_op jit(solution)/shard_map/all_gather | solution.py:209
  766.1 22.3 %reduce_sum.179 = f32[256,2048]{1,0:T(8,128)} reduce(f32[32,256,2048]{2,1,0:T(8,128)} %bitcast.158, f32[]{:T(128)} %constant.196.clone.1), dimensions={0}, to_apply=%region_27.28 | reduce | flops 16252928 | bytes 69206016 | tf_op jit(solution)/shard_map/reduce_sum | solution.py:210
  (425 shorter events, 127.7 us)
Async XLA Ops:
  7.2 12.7 %copy-start.91 = (bf16[256,1024]{1,0:T(8,128)(2,1)S(1)}, bf16[256,1024]{1,0:T(8,128)(2,1)}, u32[]{:S(2)}) copy-start(bf16[256,1024]{1,0:T(8,128)(2,1)} %param.18) | copy-start | bytes 1572868
  22.8 7.5 copy-start.114
  22.8 39.4 %all-to-all-start = ((bf16[3,16,8,2048]{3,2,0,1:T(8,128)(2,1)}), bf16[3,16,8,2048]{3,2,0,1:T(8,128)(2,1)S(1)}, u32[]{:S(2)}, u32[]{:S(2)}) async-start(bf16[3,16,8,2048]{3,2,0,1:T(8,128)(2,1)} %pad_maximum_fusion.1), calls=%async_computation | async-start | bytes 3145728 | tf_op jit(solution)/shard_map/all_to_all | solution.py:50
  68.6 14.8 %copy-start.100 = (s32[256,128]{1,0:T(8,128)S(1)}, s32[256,128]{1,0:T(8,128)}, u32[]{:S(2)}) copy-start(s32[256,128]{1,0:T(8,128)} %param.20) | copy-start | bytes 393220
  68.6 67.5 %all-to-all-start.1 = ((bf16[3,16,8,2048]{3,2,0,1:T(8,128)(2,1)}), bf16[3,16,8,2048]{3,2,0,1:T(8,128)(2,1)}, u32[]{:S(2)}, u32[]{:S(2)}) async-start(bf16[3,16,8,2048]{3,2,0,1:T(8,128)(2,1)} %copy.632), calls=%async_computation.1 | async-start | bytes 3145728 | tf_op jit(solution)/shard_map/all_to_all | solution.py:52
  77.9 151.8 %all-reduce.4.cloned.1.call-start = ((), (), s32[]{:S(2)}) async-start(), calls=%async_computation.5 | async-start | bytes 2097152 | tf_op jit(solution)/shard_map/psum | solution.py:30
  77.9 41.5 %collective-permute-start = (bf16[128,2048]{1,0:T(8,128)(2,1)}, bf16[128,2048]{1,0:T(8,128)(2,1)}, u32[]{:S(2)}, u32[]{:S(2)}) collective-permute-start(bf16[128,2048]{1,0:T(8,128)(2,1)} %get-tuple-element.112), channel_id=1, source_target_pairs={{0,1},{1,2},{2,3},{3,4},{4,5},{5,6},{6,7},{7,8},{8,9},{9,10},{10,1... | collective-permute-start | bytes 1572872 | tf_op jit(solution)/shard_map/ppermute | solution.py:22
  78.4 41.1 %collective-permute-start.1 = (bf16[128,2048]{1,0:T(8,128)(2,1)}, bf16[128,2048]{1,0:T(8,128)(2,1)}, u32[]{:S(2)}, u32[]{:S(2)}) collective-permute-start(bf16[128,2048]{1,0:T(8,128)(2,1)} %get-tuple-element.118), channel_id=1, source_target_pairs={{1,0},{2,1},{3,2},{4,3},{5,4},{6,5},{7,6},{8,7},{9,8},{10,9},{11,1... | collective-permute-start | bytes 1572872 | tf_op jit(solution)/shard_map/ppermute | solution.py:23
  83.4 682.7 %all-gather.3.cloned.1.call-start = ((), (), s32[]{:S(2)}) async-start(), calls=%async_computation.4 | async-start | bytes 69206016 | tf_op jit(solution)/shard_map/all_gather | solution.py:209
  89.7 41.2 %copy-start.59 = (bf16[2,128,256]{1,2,0:T(8,128)(2,1)}, bf16[2,128,256]{1,2,0:T(8,128)(2,1)S(1)}, u32[]{:S(2)}) copy-start(bf16[2,128,256]{1,2,0:T(8,128)(2,1)S(1)} %copy.819) | copy-start | bytes 393220
  90.6 5.9 slice-start
  92.8 39.7 %copy-start.61 = (bf16[2,128,256]{1,2,0:T(8,128)(2,1)}, bf16[2,128,256]{1,2,0:T(8,128)(2,1)S(1)}, u32[]{:S(2)}) copy-start(bf16[2,128,256]{1,2,0:T(8,128)(2,1)S(1)} %copy.825) | copy-start | bytes 393220
  122.5 8.4 %copy-start.35 = (bf16[2,384,256]{1,2,0:T(8,128)(2,1)}, bf16[2,384,256]{1,2,0:T(8,128)(2,1)S(1)}, u32[]{:S(2)}) copy-start(bf16[2,384,256]{1,2,0:T(8,128)(2,1)S(1)} %copy.624) | copy-start | bytes 1179652
  122.7 9.7 %copy-start.37 = (bf16[2,384,256]{1,2,0:T(8,128)(2,1)}, bf16[2,384,256]{1,2,0:T(8,128)(2,1)S(1)}, u32[]{:S(2)}) copy-start(bf16[2,384,256]{1,2,0:T(8,128)(2,1)S(1)} %copy.648) | copy-start | bytes 1179652
  124.1 10.0 %copy-start.39 = (bf16[2,384,256]{1,2,0:T(8,128)(2,1)}, bf16[2,384,256]{1,2,0:T(8,128)(2,1)S(1)}, u32[]{:S(2)}) copy-start(bf16[2,384,256]{1,2,0:T(8,128)(2,1)S(1)} %copy.661) | copy-start | bytes 1179652
  263.2 5.3 copy-start.43
  263.2 7.2 copy-start.15
  264.9 5.5 copy-start.13
  264.9 5.5 copy-start.33
  266.8 3.6 copy-start.11
  268.6 2.4 copy-start.9
  268.6 2.4 copy-start.109
  268.6 2.4 copy-start.110
  268.6 2.4 copy-start.111
  268.6 2.4 copy-start.112
  271.0 5.2 copy-start.3
  271.0 5.2 copy-start.45
  271.0 5.2 copy-start.55
  281.4 7.5 copy-start.107
  293.7 2.2 copy-start.19
  329.5 2.1 copy-start.85
  329.5 3.0 copy-start.86
  333.5 1.9 copy-start.89
  334.4 1.9 copy-start.90
  347.7 61.5 %all-to-all-start.2 = ((bf16[3,16,8,2048]{3,2,0,1:T(8,128)(2,1)}), bf16[3,16,8,2048]{3,2,0,1:T(8,128)(2,1)}, u32[]{:S(2)}, u32[]{:S(2)}) async-start(bf16[3,16,8,2048]{3,2,0,1:T(8,128)(2,1)} %copy.754), calls=%async_computation.2 | async-start | bytes 3145728 | tf_op jit(solution)/shard_map/all_to_all | solution.py:50
  352.5 1.9 copy-start.32
  358.3 2.3 copy-start.66
  359.2 2.7 copy-start.7
  359.2 2.7 copy-start.29
  359.2 2.7 copy-start.102
  361.9 2.3 copy-start.30
  362.8 2.1 copy-start.4
  362.8 2.1 copy-start.104
  364.9 2.3 copy-start.24
  379.7 4.9 copy-start.75
  384.6 3.6 copy-start.73
  385.7 3.6 copy-start.74
  391.6 2.6 copy-start.54
  400.7 1.9 copy-start.78
  401.0 3.1 copy-start.26
  404.8 41.6 %copy-start.16 = (f32[384,2048]{1,0:T(8,128)}, f32[384,2048]{1,0:T(8,128)S(1)}, u32[]{:S(2)}) copy-start(f32[384,2048]{1,0:T(8,128)S(1)} %fusion) | copy-start | bytes 9437188
  422.1 22.6 %copy-start.36 = (bf16[2,384,256]{1,2,0:T(8,128)(2,1)S(1)}, bf16[2,384,256]{1,2,0:T(8,128)(2,1)}, u32[]{:S(2)}) copy-start(bf16[2,384,256]{1,2,0:T(8,128)(2,1)} %copy-done.35) | copy-start | bytes 1179652
  422.1 368.4 %all-to-all-start.3 = ((bf16[3,16,8,2048]{3,2,0,1:T(8,128)(2,1)}), bf16[3,16,8,2048]{3,2,0,1:T(8,128)(2,1)}, u32[]{:S(2)}, u32[]{:S(2)}) async-start(bf16[3,16,8,2048]{3,2,0,1:T(8,128)(2,1)} %copy.758), calls=%async_computation.3 | async-start | bytes 3145728 | tf_op jit(solution)/shard_map/all_to_all | solution.py:52
  446.2 8.7 %copy-start.93 = (bf16[32,8,2,128]{3,1,2,0:T(8,128)(2,1)S(1)}, bf16[32,8,2,128]{3,1,2,0:T(8,128)(2,1)}, u32[]{:S(2)}) copy-start(bf16[32,8,2,128]{3,1,2,0:T(8,128)(2,1)} %copy.959) | copy-start | bytes 393220
  446.2 8.7 %copy-start.94 = (bf16[32,8,2,128]{3,1,2,0:T(8,128)(2,1)S(1)}, bf16[32,8,2,128]{3,1,2,0:T(8,128)(2,1)}, u32[]{:S(2)}) copy-start(bf16[32,8,2,128]{3,1,2,0:T(8,128)(2,1)} %copy.960) | copy-start | bytes 393220
  446.2 8.7 %copy-start.95 = (bf16[32,8,2,128]{3,1,2,0:T(8,128)(2,1)S(1)}, bf16[32,8,2,128]{3,1,2,0:T(8,128)(2,1)}, u32[]{:S(2)}) copy-start(bf16[32,8,2,128]{3,1,2,0:T(8,128)(2,1)} %copy.961) | copy-start | bytes 393220
  446.2 8.7 %copy-start.96 = (bf16[32,8,2,128]{3,1,2,0:T(8,128)(2,1)S(1)}, bf16[32,8,2,128]{3,1,2,0:T(8,128)(2,1)}, u32[]{:S(2)}) copy-start(bf16[32,8,2,128]{3,1,2,0:T(8,128)(2,1)} %copy.962) | copy-start | bytes 393220
  446.4 8.5 %copy-start.97 = (bf16[32,8,2,128]{3,1,2,0:T(8,128)(2,1)S(1)}, bf16[32,8,2,128]{3,1,2,0:T(8,128)(2,1)}, u32[]{:S(2)}) copy-start(bf16[32,8,2,128]{3,1,2,0:T(8,128)(2,1)} %copy.955) | copy-start | bytes 393220
  446.4 8.5 %copy-start.98 = (bf16[32,8,2,128]{3,1,2,0:T(8,128)(2,1)S(1)}, bf16[32,8,2,128]{3,1,2,0:T(8,128)(2,1)}, u32[]{:S(2)}) copy-start(bf16[32,8,2,128]{3,1,2,0:T(8,128)(2,1)} %copy.956) | copy-start | bytes 393220
  446.4 8.5 %copy-start.99 = (bf16[32,8,2,128]{3,1,2,0:T(8,128)(2,1)S(1)}, bf16[32,8,2,128]{3,1,2,0:T(8,128)(2,1)}, u32[]{:S(2)}) copy-start(bf16[32,8,2,128]{3,1,2,0:T(8,128)(2,1)} %copy.957) | copy-start | bytes 393220
  447.3 7.7 copy-start.17
  447.3 71.6 %collective-permute-start.2 = (bf16[128,2048]{1,0:T(8,128)(2,1)}, bf16[128,2048]{1,0:T(8,128)(2,1)}, u32[]{:S(2)}, u32[]{:S(2)}) collective-permute-start(bf16[128,2048]{1,0:T(8,128)(2,1)} %slice.505), channel_id=1, source_target_pairs={{0,1},{1,2},{2,3},{3,4},{4,5},{5,6},{6,7},{7,8},{8,9},{9,10},{10,1... | collective-permute-start | bytes 1572872 | tf_op jit(solution)/shard_map/ppermute | solution.py:22
  450.0 70.5 %collective-permute-start.3 = (bf16[128,2048]{1,0:T(8,128)(2,1)}, bf16[128,2048]{1,0:T(8,128)(2,1)}, u32[]{:S(2)}, u32[]{:S(2)}) collective-permute-start(bf16[128,2048]{1,0:T(8,128)(2,1)} %fusion.98), channel_id=1, source_target_pairs={{1,0},{2,1},{3,2},{4,3},{5,4},{6,5},{7,6},{8,7},{9,8},{10,9},{11,1... | collective-permute-start | bytes 1572872 | tf_op jit(solution)/shard_map/ppermute | solution.py:23
  788.4 1.9 copy-start.27
  (62 other events, 87.8 us)
Sparse Core Ops, SparseCore 0:
  84.7 144.9 all-reduce.3
  340.6 425.4 all-gather.2
